TPU v7x, 32 devices: a whole 2x2x4 slice. The times are simulated.
32 devices in a mesh: section: 2 (over core), dp: 8 (over z, x), rep: 2 (over y).
Axes of the slice: x: 2, y: 2, z: 4, core: 2. Of those that a mesh axis runs over, the one named last changes fastest.
Arguments:
- inputs: bfloat16 [4096, 1024], P(('dp', 'rep')), may hold values from -6 to 6
- cotangent: bfloat16 [4096, 1024], P(('dp', 'rep')), may hold values from -6 to 6
- seg_counts: int32 [256], P(('dp', 'rep')), may hold values from 2 to 16
- w_qkv: bfloat16 [2, 1024, 3072], P('section'), may hold values from -0.1875 to 0.1875
- w_out: bfloat16 [2, 1024, 1024], P('section'), may hold values from -0.375 to 0.375
- w_up: bfloat16 [2, 1024, 2048], P('section'), may hold values from -0.1875 to 0.1875
- w_down: bfloat16 [2, 2048, 1024], P('section'), may hold values from -0.1875 to 0.1875
- gains: float32 [2, 2, 1024], P('section'), may hold values from 0.5 to 1.5
- biases: float32 [2, 2, 1024], P('section'), may hold values from -3 to 3
Outputs:
- layer_outputs: bfloat16 [2, 4096, 1024], P('section', ('dp', 'rep'))
- input_grads: bfloat16 [2, 4096, 1024], P('section', ('dp', 'rep'))
- grad_qkv: float32 [2, 1024, 3072], P('section', 'dp')
- grad_wout: float32 [2, 1024, 1024], P('section', None, 'dp')
- grad_up: float32 [2, 1024, 2048], P('section', 'dp')
- grad_down: float32 [2, 2048, 1024], P('section', None, 'dp')
- grad_gains: float32 [2, 2, 1024], P('section', None, 'dp')
- grad_biases: float32 [2, 2, 1024], P('section', None, 'dp')
Inputs may be any that keep to these rules, and one draw needn't show every extreme that they name: seg_counts gives each series' number of valid slots; the first 16 - seg_counts slots of a series are padding.
All inputs are finite; a program needn't handle non-finite values.
Results may differ from a plain program's by a relative error of at most 0.015.
Values may be sent and summed in bfloat16 or wider, within the bound.
A program may use at most 256 MiB of HBM per device.

v0:
```python
from functools import partial
import jax
import jax.numpy as jnp
from jax import lax
from jax.sharding import PartitionSpec as P

SEG = 16
MB_SER = 8
HEAD_DIM = 128
epsilon = 1e-05


def from_behind(block, axis, distance):
    devices = range(lax.axis_size(axis))
    route = [(i - distance, i) for i in devices if i - distance in devices]
    return lax.ppermute(block, axis, route)


def normalize(hidden):
    average = jnp.mean(hidden, axis=-1, keepdims=True)
    centred = hidden - average
    inverse = lax.rsqrt(jnp.mean(centred * centred, axis=-1, keepdims=True) + epsilon)
    return (centred * inverse, inverse)


def normalize_back(grad_normed, normed, inverse):
    centre_term = jnp.mean(grad_normed, axis=-1, keepdims=True)
    slope_term = normed * jnp.mean(grad_normed * normed, axis=-1, keepdims=True)
    return inverse * (grad_normed - centre_term - slope_term)


def allowed_pairs(counts):
    number = counts.shape[0]
    rows = number * SEG
    position = jnp.broadcast_to(jnp.arange(SEG, dtype=jnp.int32)[None, :], (number, SEG)).reshape(
        rows
    )
    first = jnp.broadcast_to((SEG - counts)[:, None], (number, SEG)).reshape(rows)
    owner = jnp.broadcast_to(jnp.arange(number, dtype=jnp.int32)[:, None], (number, SEG)).reshape(
        rows
    )
    row_ids = jnp.arange(rows, dtype=jnp.int32)
    same_series = owner[:, None] == owner[None, :]
    causal = position[None, :] <= position[:, None]
    valid = (position >= first)[None, :] | (row_ids[:, None] == row_ids[None, :])
    return same_series & causal & valid


def probabilities(queries, keys_in, allowed):
    scores = jnp.einsum(
        "qhd,khd->hqk", queries, keys_in, preferred_element_type=jnp.float32
    ) * HEAD_DIM ** (-0.5)
    scores = jnp.where(allowed[None], scores, -1e30)
    largest = jnp.max(scores, axis=-1, keepdims=True)
    raised = jnp.exp(scores - largest)
    return raised / jnp.sum(raised, axis=-1, keepdims=True)


def keep_local(value):
    return value


def layer_forward(hidden_b, params, allowed, joins):
    w_qkv, w_out, w_up, w_down, gains, biases = params
    attention_join, feed_join = (joins[0], joins[1])
    rows = hidden_b.shape[0]
    local_heads = w_qkv.shape[1] // (3 * HEAD_DIM)
    hidden = hidden_b.astype(jnp.float32)
    normed_one, inverse_one = normalize(hidden)
    first_b = (normed_one * gains[0] + biases[0]).astype(jnp.bfloat16)
    packed_b = jnp.dot(first_b, w_qkv, preferred_element_type=jnp.float32).astype(jnp.bfloat16)
    split = packed_b.reshape(rows, 3, local_heads, HEAD_DIM)
    probs = probabilities(split[:, 0], split[:, 1], allowed)
    probs_b = probs.astype(jnp.bfloat16)
    mixed = jnp.einsum("hqk,khd->qhd", probs_b, split[:, 2], preferred_element_type=jnp.float32)
    mixed_b = mixed.reshape(rows, local_heads * HEAD_DIM).astype(jnp.bfloat16)
    middle = hidden + attention_join(jnp.dot(mixed_b, w_out, preferred_element_type=jnp.float32))
    normed_two, inverse_two = normalize(middle)
    second_b = (normed_two * gains[1] + biases[1]).astype(jnp.bfloat16)
    upper = jnp.dot(second_b, w_up, preferred_element_type=jnp.float32)
    active_b = jax.nn.gelu(upper, approximate=True).astype(jnp.bfloat16)
    result_b = (
        middle + feed_join(jnp.dot(active_b, w_down, preferred_element_type=jnp.float32))
    ).astype(jnp.bfloat16)
    saved = (
        normed_one,
        inverse_one,
        first_b,
        split,
        probs,
        probs_b,
        mixed_b,
        normed_two,
        inverse_two,
        second_b,
        upper,
        active_b,
    )
    return (result_b, saved)


def layer_backward(hidden_b, grad_b, params, allowed, joins):
    w_qkv, w_out, w_up, w_down, gains, biases = params
    feed_back, attention_back = (joins[2], joins[3])
    rows = hidden_b.shape[0]
    local_heads = w_qkv.shape[1] // (3 * HEAD_DIM)
    saved = layer_forward(hidden_b, params, allowed, joins)[1]
    (
        normed_one,
        inverse_one,
        first_b,
        split,
        probs,
        probs_b,
        mixed_b,
        normed_two,
        inverse_two,
        second_b,
        upper,
        active_b,
    ) = saved
    grad_result = grad_b.astype(jnp.float32)
    grad_down = jnp.einsum("rf,rd->fd", active_b, grad_b, preferred_element_type=jnp.float32)
    grad_active = jnp.einsum("rd,fd->rf", grad_b, w_down, preferred_element_type=jnp.float32)
    grad_upper = jax.vjp(partial(jax.nn.gelu, approximate=True), upper)[1](grad_active)[0]
    grad_upper_b = grad_upper.astype(jnp.bfloat16)
    grad_up = jnp.einsum("rd,rf->df", second_b, grad_upper_b, preferred_element_type=jnp.float32)
    grad_second = feed_back(
        jnp.einsum("rf,df->rd", grad_upper_b, w_up, preferred_element_type=jnp.float32)
    )
    grad_middle = grad_result + normalize_back(grad_second * gains[1], normed_two, inverse_two)
    grad_middle_b = grad_middle.astype(jnp.bfloat16)
    grad_wout = jnp.einsum("ri,ro->io", mixed_b, grad_middle_b, preferred_element_type=jnp.float32)
    grad_mixed = jnp.einsum("ro,io->ri", grad_middle_b, w_out, preferred_element_type=jnp.float32)
    grad_mixed_b = grad_mixed.astype(jnp.bfloat16).reshape(rows, local_heads, HEAD_DIM)
    grad_probs = jnp.einsum(
        "qhd,khd->hqk", grad_mixed_b, split[:, 2], preferred_element_type=jnp.float32
    )
    grad_values = jnp.einsum(
        "hqk,qhd->khd", probs_b, grad_mixed_b, preferred_element_type=jnp.float32
    )
    grad_scores = probs * (grad_probs - jnp.sum(probs * grad_probs, axis=-1, keepdims=True))
    grad_scores_b = grad_scores.astype(jnp.bfloat16)
    grad_queries = jnp.einsum(
        "hqk,khd->qhd", grad_scores_b, split[:, 1], preferred_element_type=jnp.float32
    ) * HEAD_DIM ** (-0.5)
    grad_keys = jnp.einsum(
        "hqk,qhd->khd", grad_scores_b, split[:, 0], preferred_element_type=jnp.float32
    ) * HEAD_DIM ** (-0.5)
    grad_packed = jnp.stack((grad_queries, grad_keys, grad_values), axis=1)
    grad_packed_b = grad_packed.reshape(rows, 3 * local_heads * HEAD_DIM).astype(jnp.bfloat16)
    grad_qkv = jnp.einsum("rd,re->de", first_b, grad_packed_b, preferred_element_type=jnp.float32)
    grad_first = attention_back(
        jnp.einsum("re,de->rd", grad_packed_b, w_qkv, preferred_element_type=jnp.float32)
    )
    grad_hidden = grad_middle + normalize_back(grad_first * gains[0], normed_one, inverse_one)
    grad_gains = jnp.stack(
        (jnp.sum(grad_first * normed_one, axis=0), jnp.sum(grad_second * normed_two, axis=0))
    )
    grad_biases = jnp.stack((jnp.sum(grad_first, axis=0), jnp.sum(grad_second, axis=0)))
    return (grad_hidden, (grad_qkv, grad_wout, grad_up, grad_down, grad_gains, grad_biases))


def per_device(inputs, cotangent, seg_counts, w_qkv, w_out, w_up, w_down, gains, biases):
    sections = lax.axis_size("section")
    section = lax.axis_index("section")
    rows = MB_SER * SEG
    width = inputs.shape[1]
    micro = inputs.shape[0] // rows
    ticks = micro + sections - 1
    pairs = 1
    feed_rows = inputs.reshape(micro, rows, width)
    back_rows = cotangent.reshape(micro, rows, width)
    count_rows = seg_counts.reshape(micro, MB_SER)
    params = (w_qkv[0], w_out[0], w_up[0], w_down[0], gains[0], biases[0])
    joins = (keep_local, keep_local, keep_local, keep_local)
    block_rows = pairs * rows
    zero_terms = tuple((jnp.zeros(weight.shape, jnp.float32) for weight in params))

    def forward_tick(tick, carry):
        arrived, kept, results = carry
        position = tick - section
        active = (position >= 0) & (position < micro)
        slot = jnp.clip(position, 0, micro - 1)
        source = jnp.where(section == 0, feed_rows[slot], arrived)
        allowed = allowed_pairs(count_rows[slot])
        result = lax.cond(
            active,
            lambda state: layer_forward(state, params, allowed, joins)[0],
            lambda state: jnp.zeros_like(state),
            source,
        )
        kept = jnp.where(active, lax.dynamic_update_slice_in_dim(kept, source[None], slot, 0), kept)
        results = jnp.where(
            active, lax.dynamic_update_slice_in_dim(results, result[None], slot, 0), results
        )
        arrived = from_behind(result, "section", 1)
        return (arrived, kept, results)

    empty_rows = jnp.zeros((block_rows, width), jnp.bfloat16)
    empty_store = jnp.zeros((micro, block_rows, width), jnp.bfloat16)
    _, kept, results = lax.fori_loop(0, ticks, forward_tick, (empty_rows, empty_store, empty_store))

    def backward_tick(tick, carry):
        arrived, totals, returned = carry
        position = tick - (sections - 1 - section)
        active = (position >= 0) & (position < micro)
        slot = jnp.clip(position, 0, micro - 1)
        upstream = jnp.where(section == sections - 1, back_rows[slot], arrived)
        allowed = allowed_pairs(count_rows[slot])
        layer_input = kept[slot]

        def run_layer(state):
            grad_hidden, terms = layer_backward(layer_input, state, params, allowed, joins)
            return (grad_hidden.astype(jnp.bfloat16), terms)

        def skip_layer(state):
            return (jnp.zeros_like(state), zero_terms)

        grad_hidden_b, terms = lax.cond(active, run_layer, skip_layer, upstream)
        totals = tuple((total + term for total, term in zip(totals, terms)))
        returned = jnp.where(
            active,
            lax.dynamic_update_slice_in_dim(returned, grad_hidden_b[None], slot, 0),
            returned,
        )
        arrived = from_behind(grad_hidden_b, "section", -1)
        return (arrived, totals, returned)

    _, totals, returned = lax.fori_loop(
        0, ticks, backward_tick, (empty_rows, zero_terms, empty_store)
    )
    shares = (
        lax.psum_scatter(totals[0][None], "dp", scatter_dimension=1, tiled=True),
        lax.psum_scatter(totals[1][None], "dp", scatter_dimension=2, tiled=True),
        lax.psum_scatter(totals[2][None], "dp", scatter_dimension=1, tiled=True),
        lax.psum_scatter(totals[3][None], "dp", scatter_dimension=2, tiled=True),
        lax.psum_scatter(totals[4][None], "dp", scatter_dimension=2, tiled=True),
        lax.psum_scatter(totals[5][None], "dp", scatter_dimension=2, tiled=True),
    )
    summed = (
        lax.psum(shares[0].astype(jnp.bfloat16), "rep").astype(jnp.float32),
        lax.psum(shares[1].astype(jnp.bfloat16), "rep").astype(jnp.float32),
        lax.psum(shares[2].astype(jnp.bfloat16), "rep").astype(jnp.float32),
        lax.psum(shares[3].astype(jnp.bfloat16), "rep").astype(jnp.float32),
        lax.psum(shares[4].astype(jnp.bfloat16), "rep").astype(jnp.float32),
        lax.psum(shares[5].astype(jnp.bfloat16), "rep").astype(jnp.float32),
    )
    layer_outputs = results.reshape(1, micro * rows, width)
    input_grads = returned.reshape(1, micro * rows, width)
    return (
        layer_outputs,
        input_grads,
        summed[0],
        summed[1],
        summed[2],
        summed[3],
        summed[4],
        summed[5],
    )


def solution(mesh):
    placed = (
        P(("dp", "rep"), None),
        P(("dp", "rep"), None),
        P(("dp", "rep")),
        P("section", None, None),
        P("section", None, None),
        P("section", None, None),
        P("section", None, None),
        P("section", None, None),
        P("section", None, None),
    )
    return jax.shard_map(
        per_device,
        mesh=mesh,
        in_specs=placed,
        out_specs=(
            P("section", ("dp", "rep"), None),
            P("section", ("dp", "rep"), None),
            P("section", "dp", None),
            P("section", None, "dp"),
            P("section", "dp", None),
            P("section", None, "dp"),
            P("section", None, "dp"),
            P("section", None, "dp"),
        ),
        check_vma=False,
    )
```

profile of v0, /device:TPU:0, one launch (start us, length us, event | category | flops | bytes accessed | tf_op | source)
XLA Modules:
  0.0 1205.0 jit_solution(18255057795434790949)
XLA Ops:
  9.5 80.4 %while.48 = (s32[]{:T(128)}, bf16[128,1024]{1,0:T(8,128)(2,1)S(1)}, bf16[2,128,1024]{2,1,0:T(8,128)(2,1)S(1)}, bf16[2,128,1024]{2,1,0:T(8,128)(2,1)}, s32[]{:T(1...) while((s32[]{:T(128)}, bf16[128,1024]{1,0:T(8,128)(2,1)S(1)}, ...), condition=%wide.region_9.10_spmd, body=%wide.region_0.9_spmd.sunk | while | flops 2222163456 | bytes 41540956 | solution.py:202
  10.7 22.2 %conditional.5 = (bf16[128,1024]{1,0:T(8,128)(2,1)}, bf16[1,128,1024]{2,1,0:T(8,128)(2,1)}) conditional(s32[]{:T(128)} %convert_element_type.348, () %tuple.146, (bf16[128,1024]{1,0:T(8,128)(2,1)S(1)}, f32[2,1024]{1,0:T(2,128)}, f32[2,1024]{1,0:T(2,128)}, bf16[1024,3072]{1,0:T(8,128)(2,1)}, s32[8,16]{1,0:T(8,128)S(1)}, ...), branch_computations={%region_1.1_spmd, %region_2.8_spmd} | conditional | flops 2221770240 | bytes 38262244 | solution.py:187
  37.2 22.2 %conditional.5 = (bf16[128,1024]{1,0:T(8,128)(2,1)}, bf16[1,128,1024]{2,1,0:T(8,128)(2,1)}) conditional(s32[]{:T(128)} %convert_element_type.348, () %tuple.146, (bf16[128,1024]{1,0:T(8,128)(2,1)S(1)}, f32[2,1024]{1,0:T(2,128)}, f32[2,1024]{1,0:T(2,128)}, bf16[1024,3072]{1,0:T(8,128)(2,1)}, s32[8,16]{1,0:T(8,128)S(1)}, ...), branch_computations={%region_1.1_spmd, %region_2.8_spmd} | conditional | flops 2221770240 | bytes 38262244 | solution.py:187
  65.7 22.5 %collective-permute-start = (bf16[128,1024]{1,0:T(8,128)(2,1)}, bf16[128,1024]{1,0:T(8,128)(2,1)S(1)}, u32[]{:S(2)}, u32[]{:S(2)}) collective-permute-start(bf16[128,1024]{1,0:T(8,128)(2,1)} %get-tuple-element.1496), channel_id=1, source_target_pairs={{0,16},{1,17},{2,18},{3,19},{4,20},{5,21},{6,22},{7,23},{8,24},{9,... | collective-permute-start | bytes 786440 | tf_op jit(solution)/shard_map/while/body/eval_jaxpr/ppermute | solution.py:16
  91.5 296.8 %while.49 = (s32[]{:T(128)}, bf16[128,1024]{1,0:T(8,128)(2,1)}, f32[1024,3072]{1,0:T(8,128)}, f32[1024,1024]{1,0:T(8,128)}, f32[1024,2048]{1,0:T(8,128)}, /*inde...) while((s32[]{:T(128)}, bf16[128,1024]{1,0:T(8,128)(2,1)}, ...), condition=%wide.region_28.29_spmd.clone, body=%wide.region_10.28_spmd.clone.sunk | while | flops 6145549824 | bytes 265440848 | solution.py:230
  92.1 19.7 %conditional.6 = (bf16[128,1024]{1,0:T(8,128)(2,1)}, f32[1024,3072]{1,0:T(8,128)}, f32[1024,1024]{1,0:T(8,128)}, f32[1024,2048]{1,0:T(8,128)}, f32[2048,1024]{1,...) conditional(s32[]{:T(128)} %convert_element_type.349, () %tuple.150, ...), branch_computations={%region_11.11_spmd, %region_12.27_spmd} | conditional | flops 6128633344 | bytes 157386656 | solution.py:220
  113.1 12.1 %select_add_fusion.11 = f32[1024,3072]{1,0:T(8,128)} fusion(f32[1024,3072]{1,0:T(8,128)} %get-tuple-element.1520, f32[1024,3072]{1,0:T(8,128)} %get-tuple-element.1625, pred[]{:T(512)S(6)} %compare.3), kind=kLoop, calls=%fused_computation.175.clone.1 | loop fusion | flops 6291456 | bytes 37748736 | tf_op jit(solution)/shard_map/while/body/eval_jaxpr/add | solution.py:221
  125.2 9.4 select_add_fusion.13
  134.6 9.6 select_add_fusion.14
  160.0 64.2 %conditional.6 = (bf16[128,1024]{1,0:T(8,128)(2,1)}, f32[1024,3072]{1,0:T(8,128)}, f32[1024,1024]{1,0:T(8,128)}, f32[1024,2048]{1,0:T(8,128)}, f32[2048,1024]{1,...) conditional(s32[]{:T(128)} %convert_element_type.349, () %tuple.150, ...), branch_computations={%region_11.11_spmd, %region_12.27_spmd} | conditional | flops 6128633344 | bytes 157386656 | solution.py:220
  225.5 14.9 %select_add_fusion.11 = f32[1024,3072]{1,0:T(8,128)} fusion(f32[1024,3072]{1,0:T(8,128)} %get-tuple-element.1520, f32[1024,3072]{1,0:T(8,128)} %get-tuple-element.1625, pred[]{:T(512)S(6)} %compare.3), kind=kLoop, calls=%fused_computation.175.clone.1 | loop fusion | flops 6291456 | bytes 37748736 | tf_op jit(solution)/shard_map/while/body/eval_jaxpr/add | solution.py:221
  240.5 11.8 select_add_fusion.13
  252.3 12.0 select_add_fusion.14
  274.4 64.2 %conditional.6 = (bf16[128,1024]{1,0:T(8,128)(2,1)}, f32[1024,3072]{1,0:T(8,128)}, f32[1024,1024]{1,0:T(8,128)}, f32[1024,2048]{1,0:T(8,128)}, f32[2048,1024]{1,...) conditional(s32[]{:T(128)} %convert_element_type.349, () %tuple.150, ...), branch_computations={%region_11.11_spmd, %region_12.27_spmd} | conditional | flops 6128633344 | bytes 157386656 | solution.py:220
  340.0 14.9 %select_add_fusion.11 = f32[1024,3072]{1,0:T(8,128)} fusion(f32[1024,3072]{1,0:T(8,128)} %get-tuple-element.1520, f32[1024,3072]{1,0:T(8,128)} %get-tuple-element.1625, pred[]{:T(512)S(6)} %compare.3), kind=kLoop, calls=%fused_computation.175.clone.1 | loop fusion | flops 6291456 | bytes 37748736 | tf_op jit(solution)/shard_map/while/body/eval_jaxpr/add | solution.py:221
  354.9 11.8 select_add_fusion.13
  366.7 12.0 select_add_fusion.14
  392.7 86.8 %reduce-scatter.13.cloned.1.call-done = f32[1,1024,128]{2,1,0:T(8,128)} async-done(((f32[1,1024,1024]{2,1,0:T(8,128)}), f32[1,1024,128]{2,1,0:T(8,128)}) %reduce-scatter.13.cloned.1.call-update) | async-done | bytes 524304 | tf_op jit(solution)/shard_map/reduce_scatter | solution.py:235
  481.4 151.1 %reduce-scatter.15.cloned.1.call-done = f32[1,128,2048]{2,1,0:T(8,128)} async-done(((f32[1,1024,2048]{2,1,0:T(8,128)}), f32[1,128,2048]{2,1,0:T(8,128)}) %reduce-scatter.15.cloned.1.call-update) | async-done | bytes 1048592 | tf_op jit(solution)/shard_map/reduce_scatter | solution.py:236
  634.5 150.0 %reduce-scatter.17.cloned.1.call-done = f32[1,2048,128]{2,1,0:T(8,128)} async-done(((f32[1,2048,1024]{2,1,0:T(8,128)}), f32[1,2048,128]{2,1,0:T(8,128)}) %reduce-scatter.17.cloned.1.call-update) | async-done | bytes 1048592 | tf_op jit(solution)/shard_map/reduce_scatter | solution.py:237
  786.6 208.1 %reduce-scatter.11.cloned.1.call-done = f32[1,128,3072]{2,1,0:T(8,128)} async-done(((f32[1,1024,3072]{2,1,0:T(8,128)}), f32[1,128,3072]{2,1,0:T(8,128)}) %reduce-scatter.11.cloned.1.call-update) | async-done | bytes 1572880 | tf_op jit(solution)/shard_map/reduce_scatter | solution.py:234
  997.1 62.8 %reduce-scatter.19.cloned.1.call-done = f32[128,2]{1,0:T(8,128)} async-done(((f32[1024,2]{1,0:T(8,128)}), f32[128,2]{1,0:T(8,128)}) %reduce-scatter.19.cloned.1.call-update) | async-done | bytes 1040
  1060.9 63.2 %reduce-scatter.21.cloned.1.call-done = f32[128,2]{1,0:T(8,128)} async-done(((f32[1024,2]{1,0:T(8,128)}), f32[128,2]{1,0:T(8,128)}) %reduce-scatter.21.cloned.1.call-update) | async-done | bytes 1040
  1131.1 58.7 %all-reduce.4.cloned.1.call-done = (bf16[1,128,3072]{2,1,0:T(8,128)(2,1)}, bf16[1,1024,128]{2,1,0:T(8,128)(2,1)}, bf16[1,128,2048]{2,1,0:T(8,128)(2,1)}, bf16[1,2048,128]{2,1,0:T(8,128)(2,1)}) async-done(((bf16[1,128,3072]{2,1,0:T(8,128)(2,1)}, bf16[1,1024,128]{2,1,0:T(8,128)(2,1)}, bf16[1,128,2048]{2,1,0:T(8,128)(2,1)}, bf16[1,2048,128]{2,1,0:T(8,128)(2,1)}), (bf16[1,128,3072]{2,1,0:T(8,128)(2,1)}, ...) | async-done | bytes 2097168 | tf_op jit(solution)/shard_map/psum | solution.py:242
  (380 shorter events, 279.0 us)
Async XLA Ops:
  7.2 472.4 %reduce-scatter.13.cloned.1.call-start = ((), (), s32[]{:S(2)}) async-start(), calls=%async_computation.7 | async-start | bytes 4718592 | tf_op jit(solution)/shard_map/reduce_scatter | solution.py:235
  32.9 3.1 collective-permute-start
  59.4 3.6 collective-permute-start
  65.7 24.3 %collective-permute-start = (bf16[128,1024]{1,0:T(8,128)(2,1)}, bf16[128,1024]{1,0:T(8,128)(2,1)S(1)}, u32[]{:S(2)}, u32[]{:S(2)}) collective-permute-start(bf16[128,1024]{1,0:T(8,128)(2,1)} %get-tuple-element.1496), channel_id=1, source_target_pairs={{0,16},{1,17},{2,18},{3,19},{4,20},{5,21},{6,22},{7,23},{8,24},{9,... | collective-permute-start | bytes 786440 | tf_op jit(solution)/shard_map/while/body/eval_jaxpr/ppermute | solution.py:16
  111.8 46.9 %collective-permute-start.1 = (bf16[128,1024]{1,0:T(8,128)(2,1)}, bf16[128,1024]{1,0:T(8,128)(2,1)S(1)}, u32[]{:S(2)}, u32[]{:S(2)}) collective-permute-start(bf16[128,1024]{1,0:T(8,128)(2,1)} %get-tuple-element.1519), channel_id=1, source_target_pairs={{16,0},{17,1},{18,2},{19,3},{20,4},{21,5},{22,6},{23,7},{24,8},{25... | collective-permute-start | bytes 786440 | tf_op jit(solution)/shard_map/while/body/eval_jaxpr/ppermute | solution.py:16
  150.6 8.2 copy-start.20
  165.1 10.3 copy-start.1
  165.5 16.0 %copy-start.8 = (bf16[128,1,8,128]{3,2,1,0:T(8,128)(2,1)}, bf16[128,1,8,128]{3,2,1,0:T(8,128)(2,1)S(1)}, u32[]{:S(2)}) copy-start(bf16[128,1,8,128]{3,2,1,0:T(8,128)(2,1)S(1)} %get-tuple-element.1274) | copy-start | bytes 786436 | tf_op jit(solution)/shard_map/while/body/eval_jaxpr/cond
  192.0 11.1 copy-start.16
  192.0 11.1 copy-start.18
  200.6 10.2 slice-start
  224.2 48.7 %collective-permute-start.1 = (bf16[128,1024]{1,0:T(8,128)(2,1)}, bf16[128,1024]{1,0:T(8,128)(2,1)S(1)}, u32[]{:S(2)}, u32[]{:S(2)}) collective-permute-start(bf16[128,1024]{1,0:T(8,128)(2,1)} %get-tuple-element.1519), channel_id=1, source_target_pairs={{16,0},{17,1},{18,2},{19,3},{20,4},{21,5},{22,6},{23,7},{24,8},{25... | collective-permute-start | bytes 786440 | tf_op jit(solution)/shard_map/while/body/eval_jaxpr/ppermute | solution.py:16
  279.5 10.3 copy-start.1
  279.9 16.0 %copy-start.8 = (bf16[128,1,8,128]{3,2,1,0:T(8,128)(2,1)}, bf16[128,1,8,128]{3,2,1,0:T(8,128)(2,1)S(1)}, u32[]{:S(2)}) copy-start(bf16[128,1,8,128]{3,2,1,0:T(8,128)(2,1)S(1)} %get-tuple-element.1274) | copy-start | bytes 786436 | tf_op jit(solution)/shard_map/while/body/eval_jaxpr/cond
  306.4 11.1 copy-start.16
  306.4 11.1 copy-start.18
  315.0 10.2 slice-start
  338.7 48.7 %collective-permute-start.1 = (bf16[128,1024]{1,0:T(8,128)(2,1)}, bf16[128,1024]{1,0:T(8,128)(2,1)S(1)}, u32[]{:S(2)}, u32[]{:S(2)}) collective-permute-start(bf16[128,1024]{1,0:T(8,128)(2,1)} %get-tuple-element.1519), channel_id=1, source_target_pairs={{16,0},{17,1},{18,2},{19,3},{20,4},{21,5},{22,6},{23,7},{24,8},{25... | collective-permute-start | bytes 786440 | tf_op jit(solution)/shard_map/while/body/eval_jaxpr/ppermute | solution.py:16
  388.3 244.2 %reduce-scatter.15.cloned.1.call-start = ((), (), s32[]{:S(2)}) async-start(), calls=%async_computation.8 | async-start | bytes 9437184 | tf_op jit(solution)/shard_map/reduce_scatter | solution.py:236
  389.0 395.5 %reduce-scatter.17.cloned.1.call-start = ((), (), s32[]{:S(2)}) async-start(), calls=%async_computation.9 | async-start | bytes 9437184 | tf_op jit(solution)/shard_map/reduce_scatter | solution.py:237
  389.8 605.0 %reduce-scatter.11.cloned.1.call-start = ((), (), s32[]{:S(2)}) async-start(), calls=%async_computation.6 | async-start | bytes 14155776 | tf_op jit(solution)/shard_map/reduce_scatter | solution.py:234
  390.3 669.6 %reduce-scatter.19.cloned.1.call-start = ((), (), s32[]{:S(2)}) async-start(), calls=%async_computation.10 | async-start | bytes 589824
  391.6 732.6 %reduce-scatter.21.cloned.1.call-start = ((), (), s32[]{:S(2)}) async-start(), calls=%async_computation.11 | async-start | bytes 589824
  392.7 797.1 %all-reduce.4.cloned.1.call-start = ((), (), s32[]{:S(2)}) async-start(), calls=%async_computation.12 | async-start | bytes 4194304 | tf_op jit(solution)/shard_map/psum | solution.py:242
  (54 other events, 258.8 us)
Sparse Core Ops, SparseCore 0:
  388.4 91.1 reduce-scatter.12
  483.6 148.7 reduce-scatter.14
  636.1 148.3 reduce-scatter.16
  788.4 206.2 reduce-scatter.10
  998.9 61.0 reduce-scatter.18
  1063.2 60.8 reduce-scatter.20
  1127.3 62.4 all-reduce.3
where the time goes:
time: 1210 us
  waiting for transfers between devices  791 us (65%)
  other arithmetic  180 us (15%)
  matrix products  115 us (10%)
  local copies, waits for them, and re-layouts  68.8 us (6%)
  starting transfers between devices  29.8 us (2%)
  between operations  14.2 us (1%)
    reduce_scatter x1, waiting for transfers between devices, per_device(): lax.psum_scatter(totals[0][None], 'dp', scatter_dimension=1, tiled=True)  208 us
    reduce_scatter x1, waiting for transfers between devices, per_device(): lax.psum_scatter(totals[2][None], 'dp', scatter_dimension=1, tiled=True)  151 us
    reduce_scatter x1, waiting for transfers between devices, per_device(): lax.psum_scatter(totals[3][None], 'dp', scatter_dimension=2, tiled=True)  150 us
    add x15, other arithmetic, backward_tick(): totals = tuple((total + term for total, term in zip(totals, terms)))  130 us
    unnamed x9, waiting for transfers between devices  128 us
    reduce_scatter x1, waiting for transfers between devices, per_device(): lax.psum_scatter(totals[1][None], 'dp', scatter_dimension=2, tiled=True)  86.8 us
    psum x1, waiting for transfers between devices, per_device(): lax.psum(shares[0].astype(jnp.bfloat16), 'rep').astype(jnp.float32)  58.7 us
    ppermute x6, starting transfers between devices, from_behind(): return lax.ppermute(block, axis, route)  29.5 us
  transfers between devices with their start and end apart: 13, of which 8 were waited for; matrix products, arithmetic and copies ran while one was open for 13% of the time, Pallas kernels for 0%

commit v1 on v0

--- a/solution.py
+++ b/solution.py
@@ -8,6 +8,12 @@
 MB_SER = 8
 HEAD_DIM = 128
 epsilon = 1e-05
+
+
+def gather_and_add(array, mesh_axis):
+    terms = lax.all_gather(array, mesh_axis, axis=0, tiled=False)
+    acc = terms.sum(axis=0)
+    return acc
 
 
 def from_behind(block, axis, distance):
@@ -239,7 +245,7 @@
         lax.psum_scatter(totals[5][None], "dp", scatter_dimension=2, tiled=True),
     )
     summed = (
-        lax.psum(shares[0].astype(jnp.bfloat16), "rep").astype(jnp.float32),
+        gather_and_add(shares[0].astype(jnp.bfloat16), "rep").astype(jnp.float32),
         lax.psum(shares[1].astype(jnp.bfloat16), "rep").astype(jnp.float32),
         lax.psum(shares[2].astype(jnp.bfloat16), "rep").astype(jnp.float32),
         lax.psum(shares[3].astype(jnp.bfloat16), "rep").astype(jnp.float32),

time: 1210 us -> 1210 us (level)
    all_gather x0 -> x1, waiting for transfers between devices: none -> 23.4 us  [gather_and_add(): terms = lax.all_gather(array, mesh_axis, axis=0, tiled=False)]
    psum x1, waiting for transfers between devices: 58.7 us -> 41.3 us  [per_device(): lax.psum(shares[1].astype(jnp.bfloat16), 'rep').astype(jnp.float32)]
    unnamed x9 -> x10, waiting for transfers between devices: 128 us -> 128 us
  transfers between devices with their start and end apart: 13 -> 14, of which waited for: 8 -> 9; matrix products, arithmetic and copies ran while one was open for 13% -> 13% of each run, Pallas kernels for 0% -> 0%
where the time goes in v1:
time: 1210 us
  waiting for transfers between devices  797 us (66%)
  other arithmetic  181 us (15%)
  matrix products  115 us (10%)
  local copies, waits for them, and re-layouts  68.8 us (6%)
  starting transfers between devices  29.8 us (2%)
  between operations  14.2 us (1%)
    reduce_scatter x1, waiting for transfers between devices, per_device(): lax.psum_scatter(totals[0][None], 'dp', scatter_dimension=1, tiled=True)  208 us
    reduce_scatter x1, waiting for transfers between devices, per_device(): lax.psum_scatter(totals[2][None], 'dp', scatter_dimension=1, tiled=True)  151 us
    reduce_scatter x1, waiting for transfers between devices, per_device(): lax.psum_scatter(totals[3][None], 'dp', scatter_dimension=2, tiled=True)  150 us
    add x15, other arithmetic, backward_tick(): totals = tuple((total + term for total, term in zip(totals, terms)))  130 us
    unnamed x10, waiting for transfers between devices  128 us
    reduce_scatter x1, waiting for transfers between devices, per_device(): lax.psum_scatter(totals[1][None], 'dp', scatter_dimension=2, tiled=True)  86.8 us
    psum x1, waiting for transfers between devices, per_device(): lax.psum(shares[1].astype(jnp.bfloat16), 'rep').astype(jnp.float32)  41.3 us
    ppermute x6, starting transfers between devices, from_behind(): return lax.ppermute(block, axis, route)  29.5 us
  transfers between devices with their start and end apart: 14, of which 9 were waited for; matrix products, arithmetic and copies ran while one was open for 13% of the time, Pallas kernels for 0%

profile of v1, /device:TPU:0, one launch (start us, length us, event | category | flops | bytes accessed | tf_op | source)
XLA Modules:
  0.0 1211.7 jit_solution(15860973991415784357)
XLA Ops:
  9.5 80.4 %while.48 = (s32[]{:T(128)}, bf16[128,1024]{1,0:T(8,128)(2,1)S(1)}, bf16[2,128,1024]{2,1,0:T(8,128)(2,1)S(1)}, bf16[2,128,1024]{2,1,0:T(8,128)(2,1)}, s32[]{:T(1...) while((s32[]{:T(128)}, bf16[128,1024]{1,0:T(8,128)(2,1)S(1)}, ...), condition=%wide.region_9.10_spmd, body=%wide.region_0.9_spmd.sunk | while | flops 2222163456 | bytes 41540956 | solution.py:208
  10.7 22.2 %conditional.5 = (bf16[128,1024]{1,0:T(8,128)(2,1)}, bf16[1,128,1024]{2,1,0:T(8,128)(2,1)}) conditional(s32[]{:T(128)} %convert_element_type.363, () %tuple.146, (bf16[128,1024]{1,0:T(8,128)(2,1)S(1)}, f32[2,1024]{1,0:T(2,128)}, f32[2,1024]{1,0:T(2,128)}, bf16[1024,3072]{1,0:T(8,128)(2,1)}, s32[8,16]{1,0:T(8,128)S(1)}, ...), branch_computations={%region_1.1_spmd, %region_2.8_spmd} | conditional | flops 2221770240 | bytes 38262244 | solution.py:193
  37.2 22.2 %conditional.5 = (bf16[128,1024]{1,0:T(8,128)(2,1)}, bf16[1,128,1024]{2,1,0:T(8,128)(2,1)}) conditional(s32[]{:T(128)} %convert_element_type.363, () %tuple.146, (bf16[128,1024]{1,0:T(8,128)(2,1)S(1)}, f32[2,1024]{1,0:T(2,128)}, f32[2,1024]{1,0:T(2,128)}, bf16[1024,3072]{1,0:T(8,128)(2,1)}, s32[8,16]{1,0:T(8,128)S(1)}, ...), branch_computations={%region_1.1_spmd, %region_2.8_spmd} | conditional | flops 2221770240 | bytes 38262244 | solution.py:193
  65.7 22.5 %collective-permute-start = (bf16[128,1024]{1,0:T(8,128)(2,1)}, bf16[128,1024]{1,0:T(8,128)(2,1)S(1)}, u32[]{:S(2)}, u32[]{:S(2)}) collective-permute-start(bf16[128,1024]{1,0:T(8,128)(2,1)} %get-tuple-element.1495), channel_id=1, source_target_pairs={{0,16},{1,17},{2,18},{3,19},{4,20},{5,21},{6,22},{7,23},{8,24},{9,... | collective-permute-start | bytes 786440 | tf_op jit(solution)/shard_map/while/body/eval_jaxpr/ppermute | solution.py:22
  91.5 296.8 %while.49 = (s32[]{:T(128)}, bf16[128,1024]{1,0:T(8,128)(2,1)}, f32[1024,3072]{1,0:T(8,128)}, f32[1024,1024]{1,0:T(8,128)}, f32[1024,2048]{1,0:T(8,128)}, /*inde...) while((s32[]{:T(128)}, bf16[128,1024]{1,0:T(8,128)(2,1)}, ...), condition=%wide.region_28.29_spmd.clone, body=%wide.region_10.28_spmd.clone.sunk | while | flops 6145549824 | bytes 265440848 | solution.py:236
  92.1 19.7 %conditional.6 = (bf16[128,1024]{1,0:T(8,128)(2,1)}, f32[1024,3072]{1,0:T(8,128)}, f32[1024,1024]{1,0:T(8,128)}, f32[1024,2048]{1,0:T(8,128)}, f32[2048,1024]{1,...) conditional(s32[]{:T(128)} %convert_element_type.364, () %tuple.150, ...), branch_computations={%region_11.11_spmd, %region_12.27_spmd} | conditional | flops 6128633344 | bytes 157386656 | solution.py:226
  113.1 12.1 select_add_fusion.11
  134.6 9.6 select_add_fusion.14
  160.0 64.2 %conditional.6 = (bf16[128,1024]{1,0:T(8,128)(2,1)}, f32[1024,3072]{1,0:T(8,128)}, f32[1024,1024]{1,0:T(8,128)}, f32[1024,2048]{1,0:T(8,128)}, f32[2048,1024]{1,...) conditional(s32[]{:T(128)} %convert_element_type.364, () %tuple.150, ...), branch_computations={%region_11.11_spmd, %region_12.27_spmd} | conditional | flops 6128633344 | bytes 157386656 | solution.py:226
  225.5 14.9 %select_add_fusion.11 = f32[1024,3072]{1,0:T(8,128)} fusion(f32[1024,3072]{1,0:T(8,128)} %get-tuple-element.1519, f32[1024,3072]{1,0:T(8,128)} %get-tuple-element.1624, pred[]{:T(512)S(6)} %compare.3), kind=kLoop, calls=%fused_computation.175.clone.1 | loop fusion | flops 6291456 | bytes 37748736 | tf_op jit(solution)/shard_map/while/body/eval_jaxpr/add | solution.py:227
  240.5 11.8 select_add_fusion.13
  252.3 12.0 select_add_fusion.14
  274.4 64.2 %conditional.6 = (bf16[128,1024]{1,0:T(8,128)(2,1)}, f32[1024,3072]{1,0:T(8,128)}, f32[1024,1024]{1,0:T(8,128)}, f32[1024,2048]{1,0:T(8,128)}, f32[2048,1024]{1,...) conditional(s32[]{:T(128)} %convert_element_type.364, () %tuple.150, ...), branch_computations={%region_11.11_spmd, %region_12.27_spmd} | conditional | flops 6128633344 | bytes 157386656 | solution.py:226
  340.0 14.9 %select_add_fusion.11 = f32[1024,3072]{1,0:T(8,128)} fusion(f32[1024,3072]{1,0:T(8,128)} %get-tuple-element.1519, f32[1024,3072]{1,0:T(8,128)} %get-tuple-element.1624, pred[]{:T(512)S(6)} %compare.3), kind=kLoop, calls=%fused_computation.175.clone.1 | loop fusion | flops 6291456 | bytes 37748736 | tf_op jit(solution)/shard_map/while/body/eval_jaxpr/add | solution.py:227
  354.9 11.8 select_add_fusion.13
  366.7 12.0 select_add_fusion.14
  392.7 86.8 %reduce-scatter.13.cloned.1.call-done = f32[1,1024,128]{2,1,0:T(8,128)} async-done(((f32[1,1024,1024]{2,1,0:T(8,128)}), f32[1,1024,128]{2,1,0:T(8,128)}) %reduce-scatter.13.cloned.1.call-update) | async-done | bytes 524304 | tf_op jit(solution)/shard_map/reduce_scatter | solution.py:241
  481.4 151.1 %reduce-scatter.15.cloned.1.call-done = f32[1,128,2048]{2,1,0:T(8,128)} async-done(((f32[1,1024,2048]{2,1,0:T(8,128)}), f32[1,128,2048]{2,1,0:T(8,128)}) %reduce-scatter.15.cloned.1.call-update) | async-done | bytes 1048592 | tf_op jit(solution)/shard_map/reduce_scatter | solution.py:242
  634.5 150.0 %reduce-scatter.17.cloned.1.call-done = f32[1,2048,128]{2,1,0:T(8,128)} async-done(((f32[1,2048,1024]{2,1,0:T(8,128)}), f32[1,2048,128]{2,1,0:T(8,128)}) %reduce-scatter.17.cloned.1.call-update) | async-done | bytes 1048592 | tf_op jit(solution)/shard_map/reduce_scatter | solution.py:243
  786.7 208.0 %reduce-scatter.11.cloned.1.call-done = f32[1,128,3072]{2,1,0:T(8,128)} async-done(((f32[1,1024,3072]{2,1,0:T(8,128)}), f32[1,128,3072]{2,1,0:T(8,128)}) %reduce-scatter.11.cloned.1.call-update) | async-done | bytes 1572880 | tf_op jit(solution)/shard_map/reduce_scatter | solution.py:240
  997.1 62.8 %reduce-scatter.19.cloned.1.call-done = f32[128,2]{1,0:T(8,128)} async-done(((f32[1024,2]{1,0:T(8,128)}), f32[128,2]{1,0:T(8,128)}) %reduce-scatter.19.cloned.1.call-update) | async-done | bytes 1040
  1060.9 63.2 %reduce-scatter.21.cloned.1.call-done = f32[128,2]{1,0:T(8,128)} async-done(((f32[1024,2]{1,0:T(8,128)}), f32[128,2]{1,0:T(8,128)}) %reduce-scatter.21.cloned.1.call-update) | async-done | bytes 1040
  1131.1 41.3 %all-reduce.4.cloned.1.call-done = (bf16[1,1024,128]{2,1,0:T(8,128)(2,1)}, bf16[1,128,2048]{2,1,0:T(8,128)(2,1)}, bf16[1,2048,128]{2,1,0:T(8,128)(2,1)}) async-done(((bf16[1,1024,128]{2,1,0:T(8,128)(2,1)}, bf16[1,128,2048]{2,1,0:T(8,128)(2,1)}, bf16[1,2048,128]{2,1,0:T(8,128)(2,1)}), (bf16[1,1024,128]{2,1,0:T(8,128)(2,1)}, bf16[1,128,2048]{2,1,0:T(8,128)(2,1)}, ...) | async-done | bytes 1310736 | tf_op jit(solution)/shard_map/psum | solution.py:249
  1178.4 23.4 %all-gather.3.cloned.1.call-done = bf16[2,128,3072]{2,1,0:T(8,128)(2,1)} async-done(((bf16[1,128,3072]{2,1,0:T(8,128)(2,1)}), bf16[2,128,3072]{2,1,0:T(8,128)(2,1)}) %all-gather.3.cloned.1.call-update) | async-done | bytes 1572880 | tf_op jit(solution)/shard_map/all_gather | solution.py:14
  (384 shorter events, 289.2 us)
Async XLA Ops:
  7.2 472.4 %reduce-scatter.13.cloned.1.call-start = ((), (), s32[]{:S(2)}) async-start(), calls=%async_computation.7 | async-start | bytes 4718592 | tf_op jit(solution)/shard_map/reduce_scatter | solution.py:241
  32.9 3.1 collective-permute-start
  59.4 3.6 collective-permute-start
  65.7 24.3 %collective-permute-start = (bf16[128,1024]{1,0:T(8,128)(2,1)}, bf16[128,1024]{1,0:T(8,128)(2,1)S(1)}, u32[]{:S(2)}, u32[]{:S(2)}) collective-permute-start(bf16[128,1024]{1,0:T(8,128)(2,1)} %get-tuple-element.1495), channel_id=1, source_target_pairs={{0,16},{1,17},{2,18},{3,19},{4,20},{5,21},{6,22},{7,23},{8,24},{9,... | collective-permute-start | bytes 786440 | tf_op jit(solution)/shard_map/while/body/eval_jaxpr/ppermute | solution.py:22
  111.8 46.9 %collective-permute-start.1 = (bf16[128,1024]{1,0:T(8,128)(2,1)}, bf16[128,1024]{1,0:T(8,128)(2,1)S(1)}, u32[]{:S(2)}, u32[]{:S(2)}) collective-permute-start(bf16[128,1024]{1,0:T(8,128)(2,1)} %get-tuple-element.1518), channel_id=1, source_target_pairs={{16,0},{17,1},{18,2},{19,3},{20,4},{21,5},{22,6},{23,7},{24,8},{25... | collective-permute-start | bytes 786440 | tf_op jit(solution)/shard_map/while/body/eval_jaxpr/ppermute | solution.py:22
  165.1 10.3 copy-start.1
  165.5 16.0 %copy-start.8 = (bf16[128,1,8,128]{3,2,1,0:T(8,128)(2,1)}, bf16[128,1,8,128]{3,2,1,0:T(8,128)(2,1)S(1)}, u32[]{:S(2)}) copy-start(bf16[128,1,8,128]{3,2,1,0:T(8,128)(2,1)S(1)} %get-tuple-element.1273) | copy-start | bytes 786436 | tf_op jit(solution)/shard_map/while/body/eval_jaxpr/cond
  192.0 11.1 copy-start.16
  192.0 11.1 copy-start.18
  200.6 10.2 slice-start
  224.2 48.7 %collective-permute-start.1 = (bf16[128,1024]{1,0:T(8,128)(2,1)}, bf16[128,1024]{1,0:T(8,128)(2,1)S(1)}, u32[]{:S(2)}, u32[]{:S(2)}) collective-permute-start(bf16[128,1024]{1,0:T(8,128)(2,1)} %get-tuple-element.1518), channel_id=1, source_target_pairs={{16,0},{17,1},{18,2},{19,3},{20,4},{21,5},{22,6},{23,7},{24,8},{25... | collective-permute-start | bytes 786440 | tf_op jit(solution)/shard_map/while/body/eval_jaxpr/ppermute | solution.py:22
  279.5 10.3 copy-start.1
  279.9 16.0 %copy-start.8 = (bf16[128,1,8,128]{3,2,1,0:T(8,128)(2,1)}, bf16[128,1,8,128]{3,2,1,0:T(8,128)(2,1)S(1)}, u32[]{:S(2)}) copy-start(bf16[128,1,8,128]{3,2,1,0:T(8,128)(2,1)S(1)} %get-tuple-element.1273) | copy-start | bytes 786436 | tf_op jit(solution)/shard_map/while/body/eval_jaxpr/cond
  306.4 11.1 copy-start.16
  306.4 11.1 copy-start.18
  315.0 10.2 slice-start
  338.7 48.7 %collective-permute-start.1 = (bf16[128,1024]{1,0:T(8,128)(2,1)}, bf16[128,1024]{1,0:T(8,128)(2,1)S(1)}, u32[]{:S(2)}, u32[]{:S(2)}) collective-permute-start(bf16[128,1024]{1,0:T(8,128)(2,1)} %get-tuple-element.1518), channel_id=1, source_target_pairs={{16,0},{17,1},{18,2},{19,3},{20,4},{21,5},{22,6},{23,7},{24,8},{25... | collective-permute-start | bytes 786440 | tf_op jit(solution)/shard_map/while/body/eval_jaxpr/ppermute | solution.py:22
  388.3 244.2 %reduce-scatter.15.cloned.1.call-start = ((), (), s32[]{:S(2)}) async-start(), calls=%async_computation.8 | async-start | bytes 9437184 | tf_op jit(solution)/shard_map/reduce_scatter | solution.py:242
  389.0 395.5 %reduce-scatter.17.cloned.1.call-start = ((), (), s32[]{:S(2)}) async-start(), calls=%async_computation.9 | async-start | bytes 9437184 | tf_op jit(solution)/shard_map/reduce_scatter | solution.py:243
  389.8 605.0 %reduce-scatter.11.cloned.1.call-start = ((), (), s32[]{:S(2)}) async-start(), calls=%async_computation.6 | async-start | bytes 14155776 | tf_op jit(solution)/shard_map/reduce_scatter | solution.py:240
  390.3 669.6 %reduce-scatter.19.cloned.1.call-start = ((), (), s32[]{:S(2)}) async-start(), calls=%async_computation.11 | async-start | bytes 589824
  391.6 732.6 %reduce-scatter.21.cloned.1.call-start = ((), (), s32[]{:S(2)}) async-start(), calls=%async_computation.12 | async-start | bytes 589824
  392.7 779.7 %all-reduce.4.cloned.1.call-start = ((), (), s32[]{:S(2)}) async-start(), calls=%async_computation.13 | async-start | bytes 2621440 | tf_op jit(solution)/shard_map/psum | solution.py:249
  786.6 415.2 %all-gather.3.cloned.1.call-start = ((), (), s32[]{:S(2)}) async-start(), calls=%async_computation.10 | async-start | bytes 2359296 | tf_op jit(solution)/shard_map/all_gather | solution.py:14
  (55 other events, 267.0 us)
Sparse Core Ops, SparseCore 0:
  388.4 91.1 reduce-scatter.12
  483.6 148.7 reduce-scatter.14
  636.1 148.3 reduce-scatter.16
  788.4 206.2 reduce-scatter.10
  998.9 61.0 reduce-scatter.18
  1063.2 60.8 reduce-scatter.20
  1127.3 45.1 all-reduce.3
  1174.5 27.2 all-gather.2
